TPU v7x, 512 devices: a whole 4x8x8 slice. The times are simulated.
512 devices in a mesh: gx: 64 (over z, x, core), gy: 8 (over y).
Axes of the slice: x: 4, y: 8, z: 8, core: 2. Of those that a mesh axis runs over, the one named last changes fastest.
Arguments:
- velocity: float32 [3, 128, 1536, 128], P(None, 'gx', 'gy'), may hold values from -0.8 to 2.3
- stiffness: float32 [8], P('gy'), may hold values from 100 to 100000
- block_inverse: float32 [3, 1536, 192], P(None, 'gy'), as said below
Outputs:
- velocity_next: float32 [3, 128, 1536, 128], P(None, 'gx', 'gy')
Inputs may be any that keep to these rules, and one draw needn't show every extreme that they name: block_inverse[s] for block k is, to float32 rounding, the inverse of the 192-row matrix with 1 + 2 b on its diagonal and -b beside it, b = alpha_s stiffness[k].
All inputs are finite; a program needn't handle non-finite values.
Results may differ from a plain program's by a relative error of at most 0.0003.
Values sent between devices are 32-bit elements; how exact they have to be, the bound alone decides.
No kernel may reach another device: no remote copies, remote signals or barrier semaphores. Data moves between devices by JAX's collectives and lax.ppermute only.
A program may use at most 64 MiB of HBM per device.

v0:
```python
import jax
import jax.numpy as jnp
from jax import lax
from jax.sharding import PartitionSpec as P

SUBSTEPS = 3
implicit_share = (8.0 / 15.0, 2.0 / 15.0, 1.0 / 3.0)
new_weight = (8.0 / 15.0, 5.0 / 12.0, 3.0 / 4.0)
old_weight = (0.0, -17.0 / 60.0, -5.0 / 12.0)
courant = (0.3, 0.2, 0.3)


def with_halo(cells, sides, width, closed):
    for axis, dim in sides:
        count = lax.axis_size(axis)
        ends = count if closed else count - 1
        head = lax.slice_in_dim(cells, 0, width, axis=dim)
        tail = lax.slice_in_dim(cells, cells.shape[dim] - width, cells.shape[dim], axis=dim)
        cells = jnp.concatenate(
            [
                lax.ppermute(tail, axis, [(i, (i + 1) % count) for i in range(ends)]),
                cells,
                lax.ppermute(head, axis, [((i + 1) % count, i) for i in range(ends)]),
            ],
            axis=dim,
        )
    return cells


def upwind(field, back_two, back_one, ahead_one, ahead_two, speed):
    behind = 1.5 * field - 2.0 * back_one + 0.5 * back_two
    ahead = -1.5 * field + 2.0 * ahead_one - 0.5 * ahead_two
    return jnp.maximum(speed, 0.0) * behind + jnp.minimum(speed, 0.0) * ahead


def reduced(first_vals, last_vals, tips):
    count = first_vals.shape[0]
    prev_q = jnp.zeros((), jnp.float32)
    prev_last = jnp.zeros_like(first_vals[0])
    fronts, backs, front_qs, back_qs = ([], [], [], [])
    for block in range(count):
        head_v = tips[0][block]
        tail_v = tips[1][block]
        head_w = tips[2][block]
        tail_w = tips[3][block]
        pivot = 1.0 - head_v * prev_q
        front = (first_vals[block] - head_v * prev_last) / pivot
        back = last_vals[block] - tail_v * prev_last + tail_v * prev_q * front
        front_q = head_w / pivot
        back_q = tail_w + tail_v * prev_q * front_q
        fronts.append(front)
        backs.append(back)
        front_qs.append(front_q)
        back_qs.append(back_q)
        prev_q = back_q
        prev_last = back
    heads = [None] * count
    tails = [None] * count
    heads[count - 1] = fronts[count - 1]
    tails[count - 1] = backs[count - 1]
    for block in range(count - 2, -1, -1):
        after = heads[block + 1]
        heads[block] = fronts[block] - front_qs[block] * after
        tails[block] = backs[block] - back_qs[block] * after
    zero = jnp.zeros_like(first_vals[0])
    lower_prev = jnp.stack([zero] + tails[:-1])
    upper_next = jnp.stack(heads[1:] + [zero])
    return (lower_prev, upper_next)


def body(velocity, stiffness, block_inverse):
    blocks = lax.axis_size("gy")
    own_index = lax.axis_index("gy")
    spans = velocity.shape[3]
    stiff = stiffness[0]
    first_flag = (own_index > 0).astype(jnp.float32)
    last_flag = (own_index < blocks - 1).astype(jnp.float32)
    coupling = -jnp.array(implicit_share, jnp.float32) * stiff
    lower = coupling * first_flag
    upper = coupling * last_flag
    column_v = block_inverse[:, :, 0] * lower[:, None]
    column_w = block_inverse[:, :, -1] * upper[:, None]
    own_tips = jnp.stack(
        [column_v[:, 0], column_v[:, -1], column_w[:, 0], column_w[:, -1]], axis=1
    )[:, :, None]
    every_tip = lax.all_gather(own_tips, "gy", axis=2, tiled=True)
    current = velocity
    previous = velocity
    for step in range(SUBSTEPS):
        widened = with_halo(current, (("gx", 1),), 2, True)
        middle = widened[:, 2:-2]
        ypadded = with_halo(middle, (("gy", 2),), 2, False)
        along_x = upwind(
            middle,
            widened[:, 0:-4],
            widened[:, 1:-3],
            widened[:, 3:-1],
            widened[:, 4:],
            middle[0:1],
        )
        along_y = upwind(
            middle,
            ypadded[:, :, 0:-4],
            ypadded[:, :, 1:-3],
            ypadded[:, :, 3:-1],
            ypadded[:, :, 4:],
            middle[1:2],
        )
        along_z = upwind(
            middle,
            jnp.roll(middle, 2, 3),
            jnp.roll(middle, 1, 3),
            jnp.roll(middle, -1, 3),
            jnp.roll(middle, -2, 3),
            middle[2:3],
        )
        advect = courant[0] * along_x + courant[1] * along_y + courant[2] * along_z
        diffuse = stiff * (ypadded[:, :, 3:-1] - 2.0 * middle + ypadded[:, :, 1:-3])
        forcing = middle + implicit_share[step] * diffuse - new_weight[step] * advect
        if step > 0:
            forcing = forcing - old_weight[step] * previous
        previous = advect
        planes = middle.shape[1]
        solved = jnp.einsum(
            "ij,cxjz->cxiz", block_inverse[step], forcing, precision=lax.Precision.HIGHEST
        )
        edges = jnp.stack([solved[:, :, 0, :], solved[:, :, -1, :]]).reshape(2, -1)
        tips = every_tip[step]
        grouped = lax.all_to_all(
            edges.reshape(2, blocks, -1), "gy", split_axis=1, concat_axis=1, tiled=True
        )
        lower_prev, upper_next = reduced(grouped[0], grouped[1], tips)
        returned = lax.all_to_all(
            jnp.stack([lower_prev, upper_next]), "gy", split_axis=1, concat_axis=1, tiled=True
        ).reshape(2, -1)
        lower_own = returned[0]
        upper_own = returned[1]
        lower_own = lower_own.reshape(3, planes, spans)[:, :, None, :]
        upper_own = upper_own.reshape(3, planes, spans)[:, :, None, :]
        current = (
            solved
            - column_v[step][None, None, :, None] * lower_own
            - column_w[step][None, None, :, None] * upper_own
        )
    return current


def solution(mesh):
    return jax.shard_map(
        body,
        mesh=mesh,
        in_specs=(P(None, "gx", "gy", None), P("gy"), P(None, "gy", None)),
        out_specs=P(None, "gx", "gy", None),
        check_vma=False,
    )
```

profile of v0, /device:TPU:8, one launch (start us, length us, event | category | flops | bytes accessed | tf_op | source)
XLA Modules:
  0.0 241.1 jit_solution(6409454955614664541)
XLA Ops:
  0.0 12.6 %collective-permute-start.3 = (f32[3,2,192,128]{3,2,1,0:T(8,128)}, f32[3,2,192,128]{3,2,1,0:T(8,128)}, u32[]{:S(2)}, u32[]{:S(2)}) collective-permute-start(f32[3,2,192,128]{3,2,1,0:T(8,128)} %param.4), channel_id=1, source_target_pairs={{8,0},{16,8},{24,16},{32,24},{40,32},{48,40},{56,48},{64,56},{72,6... | collective-permute-start | bytes 1769480 | tf_op jit(solution)/shard_map/ppermute | solution.py:23
  12.6 1.9 collective-permute-start.2
  14.5 0.8 fusion.335
  15.3 2.3 collective-permute-start
  17.6 3.6 %collective-permute-start.1 = (f32[3,2,2,128]{3,2,1,0:T(2,128)S(1)}, f32[3,2,2,128]{3,2,1,0:T(2,128)S(1)}, u32[]{:S(2)}, u32[]{:S(2)}) collective-permute-start(f32[3,2,2,128]{3,2,1,0:T(2,128)S(1)} %get-tuple-element.146), channel_id=1, source_target_pairs={{0,1},{1,2},{2,3},{3,4},{4,5},{5,6},{6,7},{8,9},{9,10},{10,11},{11... | collective-permute-start | bytes 18440 | tf_op jit(solution)/shard_map/ppermute | solution.py:21
  21.3 1.5 fusion.333
  23.0 1.2 fusion.331
  24.2 1.0 maximum_bitcast_fusion.8
  26.4 0.7 copy-done.20
  28.6 23.4 %all_gather.3 = f32[3,4,8]{1,0,2:T(4,128)S(1)} all-gather(f32[3,4,1]{1,0,2:T(4,128)S(1)} %maximum_bitcast_fusion.9), channel_id=1, replica_groups=mesh['gx'=64,'gy'=8] {'gy'}, dimensions={2}, use_global_device_ids=true | all-gather | bytes 432 | tf_op jit(solution)/shard_map/all_gather | solution.py:86
  52.3 0.7 fusion.339
  54.3 2.7 %fusion.61 = f32[3,2,192,128]{3,2,1,0:T(8,128)S(1)} fusion(f32[3,2,194,128]{3,2,1,0:T(8,128)S(1)} %constant_dynamic-update-slice_fusion, f32[3,2,192,128]{3,2,1,0:T(8,128)S(1)} %copy-done, f32[3,2,2,128]{3,2,1,0:T(2,128)S(1)} %copy-done.12, f32[3,2,192,128]{3,2,1,0:T(8,128)} %collective-permute-done.3, f32[3,2,192,128]{3,2,1,0:T(8,128)} %collective-permute-done.2, ...), kind=kLoop, calls=%fused_computation.79 | loop fusion | flops 7077888 | bytes 7084032 | tf_op jit(solution)/shard_map/add | solution.py:117
  57.1 1.8 convolution_bitcast_fusion.2
  59.7 5.2 %all-to-all-start = ((f32[2,8,96]{2,0,1:T(2,128)}), f32[2,8,96]{2,0,1:T(2,128)S(1)}, u32[]{:S(2)}, u32[]{:S(2)}) async-start(f32[2,8,96]{2,0,1:T(2,128)} %pad_maximum_fusion.11), calls=%async_computation | async-start | bytes 16384 | tf_op jit(solution)/shard_map/all_to_all | solution.py:129
  64.9 0.7 fusion.340
  83.8 7.7 %fusion.235 = (f32[1,96]{1,0:T(1,128)S(1)}, f32[1,96]{1,0:T(1,128)S(1)}, f32[1,96]{1,0:T(1,128)S(1)}, f32[1,96]{1,0:T(1,128)S(1)}, f32[1,96]{1,0:T(1,128)S(1)}, ...) fusion(f32[2,8,96]{2,0,1:T(2,128)S(1)} %all-to-all-done, ...), kind=kLoop, calls=%fused_computation.345 | loop fusion | flops 4512 | bytes 10476 | tf_op jit(solution)/shard_map/add | solution.py:48
  91.5 0.6 multiply_subtract_fusion.31
  92.9 7.2 %all-to-all-start.1 = ((f32[2,8,96]{2,0,1:T(2,128)}), f32[2,8,96]{2,0,1:T(2,128)S(1)}, u32[]{:S(2)}, u32[]{:S(2)}) async-start(f32[2,8,96]{2,0,1:T(2,128)} %copy.10), calls=%async_computation.1 | async-start | bytes 16384 | tf_op jit(solution)/shard_map/all_to_all | solution.py:133
  100.1 0.7 fusion.337
  100.8 5.6 %all-to-all-done.1 = f32[2,8,96]{2,0,1:T(2,128)S(1)} async-done(((f32[2,8,96]{2,0,1:T(2,128)}), f32[2,8,96]{2,0,1:T(2,128)S(1)}, u32[]{:S(2)}, u32[]{:S(2)}) %all-to-all-start.1) | async-done | bytes 6176 | tf_op jit(solution)/shard_map/all_to_all | solution.py:133
  106.6 0.7 copy-done.18
  107.4 1.9 collective-permute-start.7
  109.4 2.4 collective-permute-start.6
  112.5 3.3 %collective-permute-start.4 = (f32[3,2,2,128]{3,2,1,0:T(2,128)S(1)}, f32[3,2,2,128]{3,2,1,0:T(2,128)S(1)}, u32[]{:S(2)}, u32[]{:S(2)}) collective-permute-start(f32[3,2,2,128]{3,2,1,0:T(2,128)S(1)} %get-tuple-element.129), channel_id=1, source_target_pairs={{1,0},{2,1},{3,2},{4,3},{5,4},{6,5},{7,6},{9,8},{10,9},{11,10},{12... | collective-permute-start | bytes 18440 | tf_op jit(solution)/shard_map/ppermute | solution.py:23
  115.8 2.5 %collective-permute-start.5 = (f32[3,2,2,128]{3,2,1,0:T(2,128)S(1)}, f32[3,2,2,128]{3,2,1,0:T(2,128)S(1)}, u32[]{:S(2)}, u32[]{:S(2)}) collective-permute-start(f32[3,2,2,128]{3,2,1,0:T(2,128)S(1)} %get-tuple-element.128), channel_id=1, source_target_pairs={{0,1},{1,2},{2,3},{3,4},{4,5},{5,6},{6,7},{8,9},{9,10},{10,11},{11... | collective-permute-start | bytes 18440 | tf_op jit(solution)/shard_map/ppermute | solution.py:21
  118.6 2.7 %collective-permute-done.5 = f32[3,2,2,128]{3,2,1,0:T(2,128)S(1)} collective-permute-done((f32[3,2,2,128]{3,2,1,0:T(2,128)S(1)}, f32[3,2,2,128]{3,2,1,0:T(2,128)S(1)}, u32[]{:S(2)}, u32[]{:S(2)}) %collective-permute-start.5) | collective-permute-done | bytes 6176 | tf_op jit(solution)/shard_map/ppermute | solution.py:21
  121.3 2.5 %collective-permute-done.6 = f32[3,2,192,128]{3,2,1,0:T(8,128)S(1)} collective-permute-done((f32[3,2,192,128]{3,2,1,0:T(8,128)S(1)}, f32[3,2,192,128]{3,2,1,0:T(8,128)S(1)}, u32[]{:S(2)}, u32[]{:S(2)}) %collective-permute-start.6) | collective-permute-done | bytes 589856 | tf_op jit(solution)/shard_map/ppermute | solution.py:21
  123.9 1.3 fusion.42
  125.2 1.0 convolution_bitcast_fusion.1
  127.0 4.7 %all-to-all-start.2 = ((f32[2,8,96]{2,0,1:T(2,128)}), f32[2,8,96]{2,0,1:T(2,128)S(1)}, u32[]{:S(2)}, u32[]{:S(2)}) async-start(f32[2,8,96]{2,0,1:T(2,128)} %pad_maximum_fusion.13), calls=%async_computation.2 | async-start | bytes 16384 | tf_op jit(solution)/shard_map/all_to_all | solution.py:129
  131.7 0.7 fusion.338
  150.5 7.5 %fusion.206 = (f32[1,96]{1,0:T(1,128)S(1)}, f32[1,96]{1,0:T(1,128)S(1)}, f32[1,96]{1,0:T(1,128)S(1)}, f32[1,96]{1,0:T(1,128)S(1)}, f32[1,96]{1,0:T(1,128)S(1)}, ...) fusion(f32[2,8,96]{2,0,1:T(2,128)S(1)} %all-to-all-done.2, ...), kind=kLoop, calls=%fused_computation.301 | loop fusion | flops 4512 | bytes 10476 | tf_op jit(solution)/shard_map/add | solution.py:48
  158.8 13.3 %all_to_all.30 = f32[2,8,96]{2,0,1:T(2,128)S(1)} all-to-all(f32[2,8,96]{2,0,1:T(2,128)S(1)} %copy.13), channel_id=1, replica_groups=mesh['gx'=64,'gy'=8] {'gy'}, dimensions={1} | all-to-all | bytes 12288 | tf_op jit(solution)/shard_map/all_to_all | solution.py:133
  172.3 0.7 copy-done.16
  173.2 1.9 collective-permute-start.11
  175.1 2.4 collective-permute-start.10
  178.2 3.3 %collective-permute-start.8 = (f32[3,2,2,128]{3,2,1,0:T(2,128)S(1)}, f32[3,2,2,128]{3,2,1,0:T(2,128)S(1)}, u32[]{:S(2)}, u32[]{:S(2)}) collective-permute-start(f32[3,2,2,128]{3,2,1,0:T(2,128)S(1)} %get-tuple-element.113), channel_id=1, source_target_pairs={{1,0},{2,1},{3,2},{4,3},{5,4},{6,5},{7,6},{9,8},{10,9},{11,10},{12... | collective-permute-start | bytes 18440 | tf_op jit(solution)/shard_map/ppermute | solution.py:23
  181.5 2.7 %collective-permute-start.9 = (f32[3,2,2,128]{3,2,1,0:T(2,128)S(1)}, f32[3,2,2,128]{3,2,1,0:T(2,128)S(1)}, u32[]{:S(2)}, u32[]{:S(2)}) collective-permute-start(f32[3,2,2,128]{3,2,1,0:T(2,128)S(1)} %get-tuple-element.112), channel_id=1, source_target_pairs={{0,1},{1,2},{2,3},{3,4},{4,5},{5,6},{6,7},{8,9},{9,10},{10,11},{11... | collective-permute-start | bytes 18440 | tf_op jit(solution)/shard_map/ppermute | solution.py:21
  184.6 2.5 %collective-permute-done.9 = f32[3,2,2,128]{3,2,1,0:T(2,128)S(1)} collective-permute-done((f32[3,2,2,128]{3,2,1,0:T(2,128)S(1)}, f32[3,2,2,128]{3,2,1,0:T(2,128)S(1)}, u32[]{:S(2)}, u32[]{:S(2)}) %collective-permute-start.9) | collective-permute-done | bytes 6176 | tf_op jit(solution)/shard_map/ppermute | solution.py:21
  187.1 2.5 %collective-permute-done.10 = f32[3,2,192,128]{3,2,1,0:T(8,128)S(1)} collective-permute-done((f32[3,2,192,128]{3,2,1,0:T(8,128)S(1)}, f32[3,2,192,128]{3,2,1,0:T(8,128)S(1)}, u32[]{:S(2)}, u32[]{:S(2)}) %collective-permute-start.10) | collective-permute-done | bytes 589856 | tf_op jit(solution)/shard_map/ppermute | solution.py:21
  189.6 2.3 convolution_bitcast_fusion
  192.7 4.7 %all-to-all-start.4 = ((f32[2,8,96]{2,0,1:T(2,128)}), f32[2,8,96]{2,0,1:T(2,128)S(1)}, u32[]{:S(2)}, u32[]{:S(2)}) async-start(f32[2,8,96]{2,0,1:T(2,128)} %pad_maximum_fusion.15), calls=%async_computation.4 | async-start | bytes 16384 | tf_op jit(solution)/shard_map/all_to_all | solution.py:129
  197.4 0.7 fusion.336
  216.3 7.6 %fusion.177 = (f32[1,96]{1,0:T(1,128)S(1)}, f32[1,96]{1,0:T(1,128)S(1)}, f32[1,96]{1,0:T(1,128)S(1)}, f32[1,96]{1,0:T(1,128)S(1)}, f32[1,96]{1,0:T(1,128)S(1)}, ...) fusion(f32[2,8,96]{2,0,1:T(2,128)S(1)} %all-to-all-done.4, ...), kind=kLoop, calls=%fused_computation.257 | loop fusion | flops 4512 | bytes 10476 | tf_op jit(solution)/shard_map/add | solution.py:48
  224.6 0.7 copy-done.14
  225.3 13.3 %all_to_all.31 = f32[2,8,96]{2,0,1:T(2,128)S(1)} all-to-all(f32[2,8,96]{2,0,1:T(2,128)S(1)} %copy.16), channel_id=1, replica_groups=mesh['gx'=64,'gy'=8] {'gy'}, dimensions={1} | all-to-all | bytes 12288 | tf_op jit(solution)/shard_map/all_to_all | solution.py:133
  238.8 0.6 copy-done.15
  239.4 1.7 multiply_subtract_fusion.4
  (129 shorter events, 11.2 us)
Async XLA Ops:
  0.0 53.1 %collective-permute-start.3 = (f32[3,2,192,128]{3,2,1,0:T(8,128)}, f32[3,2,192,128]{3,2,1,0:T(8,128)}, u32[]{:S(2)}, u32[]{:S(2)}) collective-permute-start(f32[3,2,192,128]{3,2,1,0:T(8,128)} %param.4), channel_id=1, source_target_pairs={{8,0},{16,8},{24,16},{32,24},{40,32},{48,40},{56,48},{64,56},{72,6... | collective-permute-start | bytes 1769480 | tf_op jit(solution)/shard_map/ppermute | solution.py:23
  12.6 40.5 %collective-permute-start.2 = (f32[3,2,192,128]{3,2,1,0:T(8,128)}, f32[3,2,192,128]{3,2,1,0:T(8,128)}, u32[]{:S(2)}, u32[]{:S(2)}) collective-permute-start(f32[3,2,192,128]{3,2,1,0:T(8,128)} %param.4), channel_id=1, source_target_pairs={{0,8},{8,16},{16,24},{24,32},{32,40},{40,48},{48,56},{56,64},{64,7... | collective-permute-start | bytes 1769480 | tf_op jit(solution)/shard_map/ppermute | solution.py:21
  15.3 37.7 %collective-permute-start = (f32[3,2,2,128]{3,2,1,0:T(2,128)S(1)}, f32[3,2,2,128]{3,2,1,0:T(2,128)S(1)}, u32[]{:S(2)}, u32[]{:S(2)}) collective-permute-start(f32[3,2,2,128]{3,2,1,0:T(2,128)S(1)} %get-tuple-element.147), channel_id=1, source_target_pairs={{1,0},{2,1},{3,2},{4,3},{5,4},{6,5},{7,6},{9,8},{10,9},{11,10},{12... | collective-permute-start | bytes 18440 | tf_op jit(solution)/shard_map/ppermute | solution.py:23
  17.6 5.2 %copy-start = (f32[3,2,192,128]{3,2,1,0:T(8,128)S(1)}, f32[3,2,192,128]{3,2,1,0:T(8,128)}, u32[]{:S(2)}) copy-start(f32[3,2,192,128]{3,2,1,0:T(8,128)} %param.4) | copy-start | bytes 1769476
  17.6 35.4 %collective-permute-start.1 = (f32[3,2,2,128]{3,2,1,0:T(2,128)S(1)}, f32[3,2,2,128]{3,2,1,0:T(2,128)S(1)}, u32[]{:S(2)}, u32[]{:S(2)}) collective-permute-start(f32[3,2,2,128]{3,2,1,0:T(2,128)S(1)} %get-tuple-element.146), channel_id=1, source_target_pairs={{0,1},{1,2},{2,3},{3,4},{4,5},{5,6},{6,7},{8,9},{9,10},{10,11},{11... | collective-permute-start | bytes 18440 | tf_op jit(solution)/shard_map/ppermute | solution.py:21
  24.2 1.7 copy-start.3
  26.4 0.7 copy-start.20
  52.0 1.7 copy-start.1
  52.0 1.6 copy-start.2
  52.0 1.6 copy-start.5
  52.0 1.6 copy-start.6
  52.0 1.6 copy-start.7
  52.0 1.6 copy-start.8
  52.1 1.6 copy-start.9
  52.1 1.6 copy-start.10
  53.0 0.6 copy-start.11
  53.6 0.7 copy-start.12
  59.7 24.0 %all-to-all-start = ((f32[2,8,96]{2,0,1:T(2,128)}), f32[2,8,96]{2,0,1:T(2,128)S(1)}, u32[]{:S(2)}, u32[]{:S(2)}) async-start(f32[2,8,96]{2,0,1:T(2,128)} %pad_maximum_fusion.11), calls=%async_computation | async-start | bytes 16384 | tf_op jit(solution)/shard_map/all_to_all | solution.py:129
  92.2 14.4 %copy-start.19 = (f32[1,192]{1,0:T(1,128)S(1)}, f32[1,192]{1,0:T(1,128)}, u32[]{:S(2)}) copy-start(f32[1,192]{1,0:T(1,128)} %get-tuple-element.237) | copy-start | bytes 2308
  92.2 66.5 %copy-start.13 = (f32[1,96]{1,0:T(1,128)}, f32[1,96]{1,0:T(1,128)S(1)}, u32[]{:S(2)}) copy-start(f32[1,96]{1,0:T(1,128)S(1)} %broadcast.6105) | copy-start | bytes 1156
  92.9 13.5 %all-to-all-start.1 = ((f32[2,8,96]{2,0,1:T(2,128)}), f32[2,8,96]{2,0,1:T(2,128)S(1)}, u32[]{:S(2)}, u32[]{:S(2)}) async-start(f32[2,8,96]{2,0,1:T(2,128)} %copy.10), calls=%async_computation.1 | async-start | bytes 16384 | tf_op jit(solution)/shard_map/all_to_all | solution.py:133
  106.6 0.7 copy-start.18
  107.4 13.9 %collective-permute-start.7 = (f32[3,2,192,128]{3,2,1,0:T(8,128)S(1)}, f32[3,2,192,128]{3,2,1,0:T(8,128)S(1)}, u32[]{:S(2)}, u32[]{:S(2)}) collective-permute-start(f32[3,2,192,128]{3,2,1,0:T(8,128)S(1)} %multiply_subtract_fusion.6), channel_id=1, source_target_pairs={{8,0},{16,8},{24,16},{32,24},{40,32},{48,40},{56,48},{64,56},{72,6... | collective-permute-start | bytes 1769480 | tf_op jit(solution)/shard_map/ppermute | solution.py:23
  109.4 14.5 %collective-permute-start.6 = (f32[3,2,192,128]{3,2,1,0:T(8,128)S(1)}, f32[3,2,192,128]{3,2,1,0:T(8,128)S(1)}, u32[]{:S(2)}, u32[]{:S(2)}) collective-permute-start(f32[3,2,192,128]{3,2,1,0:T(8,128)S(1)} %multiply_subtract_fusion.6), channel_id=1, source_target_pairs={{0,8},{8,16},{16,24},{24,32},{32,40},{40,48},{48,56},{56,64},{64,7... | collective-permute-start | bytes 1769480 | tf_op jit(solution)/shard_map/ppermute | solution.py:21
  112.5 6.2 %collective-permute-start.4 = (f32[3,2,2,128]{3,2,1,0:T(2,128)S(1)}, f32[3,2,2,128]{3,2,1,0:T(2,128)S(1)}, u32[]{:S(2)}, u32[]{:S(2)}) collective-permute-start(f32[3,2,2,128]{3,2,1,0:T(2,128)S(1)} %get-tuple-element.129), channel_id=1, source_target_pairs={{1,0},{2,1},{3,2},{4,3},{5,4},{6,5},{7,6},{9,8},{10,9},{11,10},{12... | collective-permute-start | bytes 18440 | tf_op jit(solution)/shard_map/ppermute | solution.py:23
  115.8 5.5 %collective-permute-start.5 = (f32[3,2,2,128]{3,2,1,0:T(2,128)S(1)}, f32[3,2,2,128]{3,2,1,0:T(2,128)S(1)}, u32[]{:S(2)}, u32[]{:S(2)}) collective-permute-start(f32[3,2,2,128]{3,2,1,0:T(2,128)S(1)} %get-tuple-element.128), channel_id=1, source_target_pairs={{0,1},{1,2},{2,3},{3,4},{4,5},{5,6},{6,7},{8,9},{9,10},{10,11},{11... | collective-permute-start | bytes 18440 | tf_op jit(solution)/shard_map/ppermute | solution.py:21
  123.9 1.3 copy-start.4
  127.0 23.5 %all-to-all-start.2 = ((f32[2,8,96]{2,0,1:T(2,128)}), f32[2,8,96]{2,0,1:T(2,128)S(1)}, u32[]{:S(2)}, u32[]{:S(2)}) async-start(f32[2,8,96]{2,0,1:T(2,128)} %pad_maximum_fusion.13), calls=%async_computation.2 | async-start | bytes 16384 | tf_op jit(solution)/shard_map/all_to_all | solution.py:129
  133.7 38.6 %copy-start.17 = (f32[1,192]{1,0:T(1,128)S(1)}, f32[1,192]{1,0:T(1,128)}, u32[]{:S(2)}) copy-start(f32[1,192]{1,0:T(1,128)} %get-tuple-element.236) | copy-start | bytes 2308
  172.3 0.7 copy-start.16
  173.2 13.9 %collective-permute-start.11 = (f32[3,2,192,128]{3,2,1,0:T(8,128)S(1)}, f32[3,2,192,128]{3,2,1,0:T(8,128)S(1)}, u32[]{:S(2)}, u32[]{:S(2)}) collective-permute-start(f32[3,2,192,128]{3,2,1,0:T(8,128)S(1)} %multiply_subtract_fusion.5), channel_id=1, source_target_pairs={{8,0},{16,8},{24,16},{32,24},{40,32},{48,40},{56,48},{64,56},{72,6... | collective-permute-start | bytes 1769480 | tf_op jit(solution)/shard_map/ppermute | solution.py:23
  175.1 14.5 %collective-permute-start.10 = (f32[3,2,192,128]{3,2,1,0:T(8,128)S(1)}, f32[3,2,192,128]{3,2,1,0:T(8,128)S(1)}, u32[]{:S(2)}, u32[]{:S(2)}) collective-permute-start(f32[3,2,192,128]{3,2,1,0:T(8,128)S(1)} %multiply_subtract_fusion.5), channel_id=1, source_target_pairs={{0,8},{8,16},{16,24},{24,32},{32,40},{40,48},{48,56},{56,64},{64,7... | collective-permute-start | bytes 1769480 | tf_op jit(solution)/shard_map/ppermute | solution.py:21
  178.2 6.4 %collective-permute-start.8 = (f32[3,2,2,128]{3,2,1,0:T(2,128)S(1)}, f32[3,2,2,128]{3,2,1,0:T(2,128)S(1)}, u32[]{:S(2)}, u32[]{:S(2)}) collective-permute-start(f32[3,2,2,128]{3,2,1,0:T(2,128)S(1)} %get-tuple-element.113), channel_id=1, source_target_pairs={{1,0},{2,1},{3,2},{4,3},{5,4},{6,5},{7,6},{9,8},{10,9},{11,10},{12... | collective-permute-start | bytes 18440 | tf_op jit(solution)/shard_map/ppermute | solution.py:23
  181.5 5.5 %collective-permute-start.9 = (f32[3,2,2,128]{3,2,1,0:T(2,128)S(1)}, f32[3,2,2,128]{3,2,1,0:T(2,128)S(1)}, u32[]{:S(2)}, u32[]{:S(2)}) collective-permute-start(f32[3,2,2,128]{3,2,1,0:T(2,128)S(1)} %get-tuple-element.112), channel_id=1, source_target_pairs={{0,1},{1,2},{2,3},{3,4},{4,5},{5,6},{6,7},{8,9},{9,10},{10,11},{11... | collective-permute-start | bytes 18440 | tf_op jit(solution)/shard_map/ppermute | solution.py:21
  192.7 23.6 %all-to-all-start.4 = ((f32[2,8,96]{2,0,1:T(2,128)}), f32[2,8,96]{2,0,1:T(2,128)S(1)}, u32[]{:S(2)}, u32[]{:S(2)}) async-start(f32[2,8,96]{2,0,1:T(2,128)} %pad_maximum_fusion.15), calls=%async_computation.4 | async-start | bytes 16384 | tf_op jit(solution)/shard_map/all_to_all | solution.py:129
  224.6 0.7 copy-start.14
  238.8 0.6 copy-start.15
where the time goes:
time: 243 us; the launch traced here: 241 us
  starting transfers between devices  62.7 us (26%)
  between operations  55.7 us (23%)
  blocking collectives  50 us (21%)
  other arithmetic  34.1 us (14%)
  local copies, waits for them, and re-layouts  17.6 us (7%)
  waiting for transfers between devices  15.9 us (7%)
  matrix products  5.06 us (2%)
    all_to_all x2, blocking collectives, body(): lax.all_to_all(jnp.stack([lower_prev, upper_next]), 'gy', split_axis=1, c...  26.6 us
    ppermute x6, starting transfers between devices, with_halo(): lax.ppermute(head, axis, [((i + 1) % count, i) for i in range(ends)])  25.5 us
    all_gather x1, blocking collectives, body(): every_tip = lax.all_gather(own_tips, 'gy', axis=2, tiled=True)  23.4 us
    add x3, other arithmetic, reduced(): back = last_vals[block] - tail_v * prev_last + tail_v * prev_q * front  22.8 us
    ppermute x6, starting transfers between devices, with_halo(): lax.ppermute(tail, axis, [(i, (i + 1) % count) for i in range(ends)])  15.5 us
    all_to_all x3, starting transfers between devices, body(): lax.all_to_all(edges.reshape(2, blocks, -1), 'gy', split_axis=1, concat_a...  14.6 us
    ppermute x6, waiting for transfers between devices, with_halo(): lax.ppermute(tail, axis, [(i, (i + 1) % count) for i in range(ends)])  10.3 us
    all_to_all x1, starting transfers between devices, body(): lax.all_to_all(jnp.stack([lower_prev, upper_next]), 'gy', split_axis=1, c...  7.21 us
  transfers between devices with their start and end apart: 16, of which 5 were waited for; matrix products, arithmetic and copies ran while one was open for 5% of the time, Pallas kernels for 0%

commit v1 on v0

--- a/solution.py
+++ b/solution.py
@@ -130,8 +130,16 @@
             edges.reshape(2, blocks, -1), "gy", split_axis=1, concat_axis=1, tiled=True
         )
         lower_prev, upper_next = reduced(grouped[0], grouped[1], tips)
-        returned = lax.all_to_all(
-            jnp.stack([lower_prev, upper_next]), "gy", split_axis=1, concat_axis=1, tiled=True
+        returned = jnp.concatenate(
+            lax.all_to_all(
+                jnp.stack(
+                    jnp.split(jnp.stack([lower_prev, upper_next]), lax.axis_size("gy"), axis=1)
+                ),
+                "gy",
+                0,
+                0,
+            ),
+            axis=1,
         ).reshape(2, -1)
         lower_own = returned[0]
         upper_own = returned[1]

time: 243 us -> 247 us (1.016)
  local copies, waits for them, and re-layouts: 17.6 us -> 21.6 us
    unnamed x44 -> x65, local copies, waits for them, and re-layouts: 4.78 us -> 8.82 us
where the time goes in v1:
time: 247 us; the launch traced here: 245 us
  starting transfers between devices  62.7 us (25%)
  between operations  55.5 us (22%)
  blocking collectives  50 us (20%)
  other arithmetic  34 us (14%)
  local copies, waits for them, and re-layouts  21.6 us (9%)
  waiting for transfers between devices  15.9 us (6%)
  matrix products  5.06 us (2%)
    all_to_all x2, blocking collectives, body(): lax.all_to_all(jnp.stack(jnp.split(jnp.stack([lower_prev, upper_next]), l...  26.6 us
    ppermute x6, starting transfers between devices, with_halo(): lax.ppermute(head, axis, [((i + 1) % count, i) for i in range(ends)])  25.5 us
    all_gather x1, blocking collectives, body(): every_tip = lax.all_gather(own_tips, 'gy', axis=2, tiled=True)  23.4 us
    add x3, other arithmetic, reduced(): back = last_vals[block] - tail_v * prev_last + tail_v * prev_q * front  22.6 us
    ppermute x6, starting transfers between devices, with_halo(): lax.ppermute(tail, axis, [(i, (i + 1) % count) for i in range(ends)])  15.5 us
    all_to_all x3, starting transfers between devices, body(): lax.all_to_all(edges.reshape(2, blocks, -1), 'gy', split_axis=1, concat_a...  14.6 us
    ppermute x6, waiting for transfers between devices, with_halo(): lax.ppermute(tail, axis, [(i, (i + 1) % count) for i in range(ends)])  10.3 us
    unnamed x65, local copies, waits for them, and re-layouts  8.82 us
  transfers between devices with their start and end apart: 16, of which 5 were waited for; matrix products, arithmetic and copies ran while one was open for 5% of the time, Pallas kernels for 0%

profile of v1, /device:TPU:8, one launch (start us, length us, event | category | flops | bytes accessed | tf_op | source)
XLA Modules:
  0.0 244.8 jit_solution(14800359754178931780)
XLA Ops:
  0.0 12.6 %collective-permute-start.3 = (f32[3,2,192,128]{3,2,1,0:T(8,128)}, f32[3,2,192,128]{3,2,1,0:T(8,128)}, u32[]{:S(2)}, u32[]{:S(2)}) collective-permute-start(f32[3,2,192,128]{3,2,1,0:T(8,128)} %param.4), channel_id=1, source_target_pairs={{8,0},{16,8},{24,16},{32,24},{40,32},{48,40},{56,48},{64,56},{72,6... | collective-permute-start | bytes 1769480 | tf_op jit(solution)/shard_map/ppermute | solution.py:23
  12.6 1.9 collective-permute-start.2
  14.5 0.8 fusion.356
  15.3 2.3 collective-permute-start
  17.6 3.6 %collective-permute-start.1 = (f32[3,2,2,128]{3,2,1,0:T(2,128)S(1)}, f32[3,2,2,128]{3,2,1,0:T(2,128)S(1)}, u32[]{:S(2)}, u32[]{:S(2)}) collective-permute-start(f32[3,2,2,128]{3,2,1,0:T(2,128)S(1)} %get-tuple-element.146), channel_id=1, source_target_pairs={{0,1},{1,2},{2,3},{3,4},{4,5},{5,6},{6,7},{8,9},{9,10},{10,11},{11... | collective-permute-start | bytes 18440 | tf_op jit(solution)/shard_map/ppermute | solution.py:21
  21.3 1.5 fusion.354
  23.0 1.2 fusion.352
  24.2 1.0 maximum_bitcast_fusion.8
  26.4 0.7 copy-done.20
  28.6 23.4 %all_gather.3 = f32[3,4,8]{1,0,2:T(4,128)S(1)} all-gather(f32[3,4,1]{1,0,2:T(4,128)S(1)} %maximum_bitcast_fusion.9), channel_id=1, replica_groups=mesh['gx'=64,'gy'=8] {'gy'}, dimensions={2}, use_global_device_ids=true | all-gather | bytes 432 | tf_op jit(solution)/shard_map/all_gather | solution.py:86
  52.3 0.7 fusion.360
  54.3 2.7 %fusion.61 = f32[3,2,192,128]{3,2,1,0:T(8,128)S(1)} fusion(f32[3,2,194,128]{3,2,1,0:T(8,128)S(1)} %constant_dynamic-update-slice_fusion, f32[3,2,192,128]{3,2,1,0:T(8,128)S(1)} %copy-done, f32[3,2,2,128]{3,2,1,0:T(2,128)S(1)} %copy-done.12, f32[3,2,192,128]{3,2,1,0:T(8,128)} %collective-permute-done.3, f32[3,2,192,128]{3,2,1,0:T(8,128)} %collective-permute-done.2, ...), kind=kLoop, calls=%fused_computation.79 | loop fusion | flops 7077888 | bytes 7084032 | tf_op jit(solution)/shard_map/add | solution.py:117
  57.0 1.8 convolution_bitcast_fusion.2
  59.7 5.2 %all-to-all-start = ((f32[2,8,96]{2,0,1:T(2,128)}), f32[2,8,96]{2,0,1:T(2,128)S(1)}, u32[]{:S(2)}, u32[]{:S(2)}) async-start(f32[2,8,96]{2,0,1:T(2,128)} %pad_maximum_fusion.11), calls=%async_computation | async-start | bytes 16384 | tf_op jit(solution)/shard_map/all_to_all | solution.py:129
  64.9 0.7 fusion.361
  83.5 7.5 %fusion.256 = (f32[1,96]{1,0:T(1,128)S(1)}, f32[1,96]{1,0:T(1,128)S(1)}, f32[1,96]{1,0:T(1,128)S(1)}, f32[1,96]{1,0:T(1,128)S(1)}, f32[1,96]{1,0:T(1,128)S(1)}, ...) fusion(f32[2,8,96]{2,0,1:T(2,128)S(1)} %all-to-all-done, ...), kind=kLoop, calls=%fused_computation.432 | loop fusion | flops 4512 | bytes 10476 | tf_op jit(solution)/shard_map/add | solution.py:48
  96.3 7.2 %all-to-all-start.1 = ((f32[8,2,1,96]{3,1,2,0:T(2,128)}), f32[8,2,1,96]{3,1,2,0:T(2,128)S(1)}, u32[]{:S(2)}, u32[]{:S(2)}) async-start(f32[8,2,1,96]{3,1,2,0:T(2,128)} %constant_dynamic-update-slice_fusion.2), calls=%async_computation.1 | async-start | bytes 16384 | tf_op jit(solution)/shard_map/all_to_all | solution.py:134
  103.5 0.7 fusion.358
  104.2 5.6 %all-to-all-done.1 = f32[8,2,1,96]{3,1,2,0:T(2,128)S(1)} async-done(((f32[8,2,1,96]{3,1,2,0:T(2,128)}), f32[8,2,1,96]{3,1,2,0:T(2,128)S(1)}, u32[]{:S(2)}, u32[]{:S(2)}) %all-to-all-start.1) | async-done | bytes 6176 | tf_op jit(solution)/shard_map/all_to_all | solution.py:134
  110.0 0.7 copy-done.18
  110.8 1.9 collective-permute-start.7
  112.7 2.4 collective-permute-start.6
  115.8 3.3 %collective-permute-start.4 = (f32[3,2,2,128]{3,2,1,0:T(2,128)S(1)}, f32[3,2,2,128]{3,2,1,0:T(2,128)S(1)}, u32[]{:S(2)}, u32[]{:S(2)}) collective-permute-start(f32[3,2,2,128]{3,2,1,0:T(2,128)S(1)} %get-tuple-element.129), channel_id=1, source_target_pairs={{1,0},{2,1},{3,2},{4,3},{5,4},{6,5},{7,6},{9,8},{10,9},{11,10},{12... | collective-permute-start | bytes 18440 | tf_op jit(solution)/shard_map/ppermute | solution.py:23
  119.2 2.5 %collective-permute-start.5 = (f32[3,2,2,128]{3,2,1,0:T(2,128)S(1)}, f32[3,2,2,128]{3,2,1,0:T(2,128)S(1)}, u32[]{:S(2)}, u32[]{:S(2)}) collective-permute-start(f32[3,2,2,128]{3,2,1,0:T(2,128)S(1)} %get-tuple-element.128), channel_id=1, source_target_pairs={{0,1},{1,2},{2,3},{3,4},{4,5},{5,6},{6,7},{8,9},{9,10},{10,11},{11... | collective-permute-start | bytes 18440 | tf_op jit(solution)/shard_map/ppermute | solution.py:21
  122.0 2.7 %collective-permute-done.5 = f32[3,2,2,128]{3,2,1,0:T(2,128)S(1)} collective-permute-done((f32[3,2,2,128]{3,2,1,0:T(2,128)S(1)}, f32[3,2,2,128]{3,2,1,0:T(2,128)S(1)}, u32[]{:S(2)}, u32[]{:S(2)}) %collective-permute-start.5) | collective-permute-done | bytes 6176 | tf_op jit(solution)/shard_map/ppermute | solution.py:21
  124.7 2.5 %collective-permute-done.6 = f32[3,2,192,128]{3,2,1,0:T(8,128)S(1)} collective-permute-done((f32[3,2,192,128]{3,2,1,0:T(8,128)S(1)}, f32[3,2,192,128]{3,2,1,0:T(8,128)S(1)}, u32[]{:S(2)}, u32[]{:S(2)}) %collective-permute-start.6) | collective-permute-done | bytes 589856 | tf_op jit(solution)/shard_map/ppermute | solution.py:21
  127.3 1.3 fusion.42
  128.6 1.0 convolution_bitcast_fusion.1
  130.4 4.7 %all-to-all-start.2 = ((f32[2,8,96]{2,0,1:T(2,128)}), f32[2,8,96]{2,0,1:T(2,128)S(1)}, u32[]{:S(2)}, u32[]{:S(2)}) async-start(f32[2,8,96]{2,0,1:T(2,128)} %pad_maximum_fusion.12), calls=%async_computation.2 | async-start | bytes 16384 | tf_op jit(solution)/shard_map/all_to_all | solution.py:129
  135.0 0.7 fusion.359
  154.0 7.6 %fusion.227 = (f32[1,96]{1,0:T(1,128)S(1)}, f32[1,96]{1,0:T(1,128)S(1)}, f32[1,96]{1,0:T(1,128)S(1)}, f32[1,96]{1,0:T(1,128)S(1)}, f32[1,96]{1,0:T(1,128)S(1)}, ...) fusion(f32[2,8,96]{2,0,1:T(2,128)S(1)} %all-to-all-done.2, ...), kind=kLoop, calls=%fused_computation.388 | loop fusion | flops 4512 | bytes 10476 | tf_op jit(solution)/shard_map/add | solution.py:48
  161.6 0.7 multiply_subtract_fusion.19
  162.6 13.3 %all_to_all.30 = f32[8,2,1,96]{3,1,2,0:T(2,128)S(1)} all-to-all(f32[8,2,1,96]{3,1,2,0:T(2,128)S(1)} %constant_dynamic-update-slice_fusion.10), channel_id=1, replica_groups=mesh['gx'=64,'gy'=8] {'gy'}, dimensions={0} | all-to-all | bytes 12288 | tf_op jit(solution)/shard_map/all_to_all | solution.py:134
  176.1 0.7 copy-done.16
  177.0 1.9 collective-permute-start.11
  178.9 2.4 collective-permute-start.10
  182.0 3.3 %collective-permute-start.8 = (f32[3,2,2,128]{3,2,1,0:T(2,128)S(1)}, f32[3,2,2,128]{3,2,1,0:T(2,128)S(1)}, u32[]{:S(2)}, u32[]{:S(2)}) collective-permute-start(f32[3,2,2,128]{3,2,1,0:T(2,128)S(1)} %get-tuple-element.113), channel_id=1, source_target_pairs={{1,0},{2,1},{3,2},{4,3},{5,4},{6,5},{7,6},{9,8},{10,9},{11,10},{12... | collective-permute-start | bytes 18440 | tf_op jit(solution)/shard_map/ppermute | solution.py:23
  185.3 2.7 %collective-permute-start.9 = (f32[3,2,2,128]{3,2,1,0:T(2,128)S(1)}, f32[3,2,2,128]{3,2,1,0:T(2,128)S(1)}, u32[]{:S(2)}, u32[]{:S(2)}) collective-permute-start(f32[3,2,2,128]{3,2,1,0:T(2,128)S(1)} %get-tuple-element.112), channel_id=1, source_target_pairs={{0,1},{1,2},{2,3},{3,4},{4,5},{5,6},{6,7},{8,9},{9,10},{10,11},{11... | collective-permute-start | bytes 18440 | tf_op jit(solution)/shard_map/ppermute | solution.py:21
  188.4 2.5 %collective-permute-done.9 = f32[3,2,2,128]{3,2,1,0:T(2,128)S(1)} collective-permute-done((f32[3,2,2,128]{3,2,1,0:T(2,128)S(1)}, f32[3,2,2,128]{3,2,1,0:T(2,128)S(1)}, u32[]{:S(2)}, u32[]{:S(2)}) %collective-permute-start.9) | collective-permute-done | bytes 6176 | tf_op jit(solution)/shard_map/ppermute | solution.py:21
  190.9 2.5 %collective-permute-done.10 = f32[3,2,192,128]{3,2,1,0:T(8,128)S(1)} collective-permute-done((f32[3,2,192,128]{3,2,1,0:T(8,128)S(1)}, f32[3,2,192,128]{3,2,1,0:T(8,128)S(1)}, u32[]{:S(2)}, u32[]{:S(2)}) %collective-permute-start.10) | collective-permute-done | bytes 589856 | tf_op jit(solution)/shard_map/ppermute | solution.py:21
  193.4 2.3 convolution_bitcast_fusion
  196.5 4.7 %all-to-all-start.4 = ((f32[2,8,96]{2,0,1:T(2,128)}), f32[2,8,96]{2,0,1:T(2,128)S(1)}, u32[]{:S(2)}, u32[]{:S(2)}) async-start(f32[2,8,96]{2,0,1:T(2,128)} %pad_maximum_fusion.13), calls=%async_computation.4 | async-start | bytes 16384 | tf_op jit(solution)/shard_map/all_to_all | solution.py:129
  201.2 0.7 fusion.357
  219.9 7.5 %fusion.198 = (f32[1,96]{1,0:T(1,128)S(1)}, f32[1,96]{1,0:T(1,128)S(1)}, f32[1,96]{1,0:T(1,128)S(1)}, f32[1,96]{1,0:T(1,128)S(1)}, f32[1,96]{1,0:T(1,128)S(1)}, ...) fusion(f32[2,8,96]{2,0,1:T(2,128)S(1)} %all-to-all-done.4, ...), kind=kLoop, calls=%fused_computation.344 | loop fusion | flops 4512 | bytes 10476 | tf_op jit(solution)/shard_map/add | solution.py:48
  227.4 0.7 multiply_subtract_fusion.7
  228.9 13.3 %all_to_all.31 = f32[8,2,1,96]{3,1,2,0:T(2,128)S(1)} all-to-all(f32[8,2,1,96]{3,1,2,0:T(2,128)S(1)} %constant_dynamic-update-slice_fusion.18), channel_id=1, replica_groups=mesh['gx'=64,'gy'=8] {'gy'}, dimensions={0} | all-to-all | bytes 12288 | tf_op jit(solution)/shard_map/all_to_all | solution.py:134
  242.4 0.7 copy-done.15
  243.1 1.7 multiply_subtract_fusion.4
  (150 shorter events, 15.2 us)
Async XLA Ops:
  0.0 53.0 %collective-permute-start.3 = (f32[3,2,192,128]{3,2,1,0:T(8,128)}, f32[3,2,192,128]{3,2,1,0:T(8,128)}, u32[]{:S(2)}, u32[]{:S(2)}) collective-permute-start(f32[3,2,192,128]{3,2,1,0:T(8,128)} %param.4), channel_id=1, source_target_pairs={{8,0},{16,8},{24,16},{32,24},{40,32},{48,40},{56,48},{64,56},{72,6... | collective-permute-start | bytes 1769480 | tf_op jit(solution)/shard_map/ppermute | solution.py:23
  12.6 40.4 %collective-permute-start.2 = (f32[3,2,192,128]{3,2,1,0:T(8,128)}, f32[3,2,192,128]{3,2,1,0:T(8,128)}, u32[]{:S(2)}, u32[]{:S(2)}) collective-permute-start(f32[3,2,192,128]{3,2,1,0:T(8,128)} %param.4), channel_id=1, source_target_pairs={{0,8},{8,16},{16,24},{24,32},{32,40},{40,48},{48,56},{56,64},{64,7... | collective-permute-start | bytes 1769480 | tf_op jit(solution)/shard_map/ppermute | solution.py:21
  15.3 37.7 %collective-permute-start = (f32[3,2,2,128]{3,2,1,0:T(2,128)S(1)}, f32[3,2,2,128]{3,2,1,0:T(2,128)S(1)}, u32[]{:S(2)}, u32[]{:S(2)}) collective-permute-start(f32[3,2,2,128]{3,2,1,0:T(2,128)S(1)} %get-tuple-element.147), channel_id=1, source_target_pairs={{1,0},{2,1},{3,2},{4,3},{5,4},{6,5},{7,6},{9,8},{10,9},{11,10},{12... | collective-permute-start | bytes 18440 | tf_op jit(solution)/shard_map/ppermute | solution.py:23
  17.6 5.2 %copy-start = (f32[3,2,192,128]{3,2,1,0:T(8,128)S(1)}, f32[3,2,192,128]{3,2,1,0:T(8,128)}, u32[]{:S(2)}) copy-start(f32[3,2,192,128]{3,2,1,0:T(8,128)} %param.4) | copy-start | bytes 1769476
  17.6 35.4 %collective-permute-start.1 = (f32[3,2,2,128]{3,2,1,0:T(2,128)S(1)}, f32[3,2,2,128]{3,2,1,0:T(2,128)S(1)}, u32[]{:S(2)}, u32[]{:S(2)}) collective-permute-start(f32[3,2,2,128]{3,2,1,0:T(2,128)S(1)} %get-tuple-element.146), channel_id=1, source_target_pairs={{0,1},{1,2},{2,3},{3,4},{4,5},{5,6},{6,7},{8,9},{9,10},{10,11},{11... | collective-permute-start | bytes 18440 | tf_op jit(solution)/shard_map/ppermute | solution.py:21
  24.2 1.7 copy-start.3
  26.4 0.7 copy-start.20
  52.0 1.6 copy-start.1
  52.0 1.6 copy-start.2
  52.0 1.6 copy-start.5
  52.0 1.6 copy-start.6
  52.0 1.6 copy-start.7
  52.0 1.6 copy-start.8
  52.0 1.6 copy-start.9
  52.0 1.6 copy-start.10
  53.0 0.6 copy-start.11
  53.6 0.7 copy-start.12
  59.7 23.8 %all-to-all-start = ((f32[2,8,96]{2,0,1:T(2,128)}), f32[2,8,96]{2,0,1:T(2,128)S(1)}, u32[]{:S(2)}, u32[]{:S(2)}) async-start(f32[2,8,96]{2,0,1:T(2,128)} %pad_maximum_fusion.11), calls=%async_computation | async-start | bytes 16384 | tf_op jit(solution)/shard_map/all_to_all | solution.py:129
  91.7 70.8 %copy-start.13 = (f32[1,96]{1,0:T(1,128)}, f32[1,96]{1,0:T(1,128)S(1)}, u32[]{:S(2)}) copy-start(f32[1,96]{1,0:T(1,128)S(1)} %broadcast.6105) | copy-start | bytes 1156
  91.7 18.3 %copy-start.19 = (f32[1,192]{1,0:T(1,128)S(1)}, f32[1,192]{1,0:T(1,128)}, u32[]{:S(2)}) copy-start(f32[1,192]{1,0:T(1,128)} %get-tuple-element.261) | copy-start | bytes 2308
  96.3 13.5 %all-to-all-start.1 = ((f32[8,2,1,96]{3,1,2,0:T(2,128)}), f32[8,2,1,96]{3,1,2,0:T(2,128)S(1)}, u32[]{:S(2)}, u32[]{:S(2)}) async-start(f32[8,2,1,96]{3,1,2,0:T(2,128)} %constant_dynamic-update-slice_fusion.2), calls=%async_computation.1 | async-start | bytes 16384 | tf_op jit(solution)/shard_map/all_to_all | solution.py:134
  110.0 0.7 copy-start.18
  110.8 13.9 %collective-permute-start.7 = (f32[3,2,192,128]{3,2,1,0:T(8,128)S(1)}, f32[3,2,192,128]{3,2,1,0:T(8,128)S(1)}, u32[]{:S(2)}, u32[]{:S(2)}) collective-permute-start(f32[3,2,192,128]{3,2,1,0:T(8,128)S(1)} %multiply_subtract_fusion.6), channel_id=1, source_target_pairs={{8,0},{16,8},{24,16},{32,24},{40,32},{48,40},{56,48},{64,56},{72,6... | collective-permute-start | bytes 1769480 | tf_op jit(solution)/shard_map/ppermute | solution.py:23
  112.7 14.5 %collective-permute-start.6 = (f32[3,2,192,128]{3,2,1,0:T(8,128)S(1)}, f32[3,2,192,128]{3,2,1,0:T(8,128)S(1)}, u32[]{:S(2)}, u32[]{:S(2)}) collective-permute-start(f32[3,2,192,128]{3,2,1,0:T(8,128)S(1)} %multiply_subtract_fusion.6), channel_id=1, source_target_pairs={{0,8},{8,16},{16,24},{24,32},{32,40},{40,48},{48,56},{56,64},{64,7... | collective-permute-start | bytes 1769480 | tf_op jit(solution)/shard_map/ppermute | solution.py:21
  115.8 6.2 %collective-permute-start.4 = (f32[3,2,2,128]{3,2,1,0:T(2,128)S(1)}, f32[3,2,2,128]{3,2,1,0:T(2,128)S(1)}, u32[]{:S(2)}, u32[]{:S(2)}) collective-permute-start(f32[3,2,2,128]{3,2,1,0:T(2,128)S(1)} %get-tuple-element.129), channel_id=1, source_target_pairs={{1,0},{2,1},{3,2},{4,3},{5,4},{6,5},{7,6},{9,8},{10,9},{11,10},{12... | collective-permute-start | bytes 18440 | tf_op jit(solution)/shard_map/ppermute | solution.py:23
  119.2 5.5 %collective-permute-start.5 = (f32[3,2,2,128]{3,2,1,0:T(2,128)S(1)}, f32[3,2,2,128]{3,2,1,0:T(2,128)S(1)}, u32[]{:S(2)}, u32[]{:S(2)}) collective-permute-start(f32[3,2,2,128]{3,2,1,0:T(2,128)S(1)} %get-tuple-element.128), channel_id=1, source_target_pairs={{0,1},{1,2},{2,3},{3,4},{4,5},{5,6},{6,7},{8,9},{9,10},{10,11},{11... | collective-permute-start | bytes 18440 | tf_op jit(solution)/shard_map/ppermute | solution.py:21
  127.3 1.3 copy-start.4
  130.4 23.6 %all-to-all-start.2 = ((f32[2,8,96]{2,0,1:T(2,128)}), f32[2,8,96]{2,0,1:T(2,128)S(1)}, u32[]{:S(2)}, u32[]{:S(2)}) async-start(f32[2,8,96]{2,0,1:T(2,128)} %pad_maximum_fusion.12), calls=%async_computation.2 | async-start | bytes 16384 | tf_op jit(solution)/shard_map/all_to_all | solution.py:129
  139.5 36.6 %copy-start.17 = (f32[1,192]{1,0:T(1,128)S(1)}, f32[1,192]{1,0:T(1,128)}, u32[]{:S(2)}) copy-start(f32[1,192]{1,0:T(1,128)} %get-tuple-element.260) | copy-start | bytes 2308
  176.1 0.7 copy-start.16
  177.0 13.9 %collective-permute-start.11 = (f32[3,2,192,128]{3,2,1,0:T(8,128)S(1)}, f32[3,2,192,128]{3,2,1,0:T(8,128)S(1)}, u32[]{:S(2)}, u32[]{:S(2)}) collective-permute-start(f32[3,2,192,128]{3,2,1,0:T(8,128)S(1)} %multiply_subtract_fusion.5), channel_id=1, source_target_pairs={{8,0},{16,8},{24,16},{32,24},{40,32},{48,40},{56,48},{64,56},{72,6... | collective-permute-start | bytes 1769480 | tf_op jit(solution)/shard_map/ppermute | solution.py:23
  178.9 14.5 %collective-permute-start.10 = (f32[3,2,192,128]{3,2,1,0:T(8,128)S(1)}, f32[3,2,192,128]{3,2,1,0:T(8,128)S(1)}, u32[]{:S(2)}, u32[]{:S(2)}) collective-permute-start(f32[3,2,192,128]{3,2,1,0:T(8,128)S(1)} %multiply_subtract_fusion.5), channel_id=1, source_target_pairs={{0,8},{8,16},{16,24},{24,32},{32,40},{40,48},{48,56},{56,64},{64,7... | collective-permute-start | bytes 1769480 | tf_op jit(solution)/shard_map/ppermute | solution.py:21
  182.0 6.4 %collective-permute-start.8 = (f32[3,2,2,128]{3,2,1,0:T(2,128)S(1)}, f32[3,2,2,128]{3,2,1,0:T(2,128)S(1)}, u32[]{:S(2)}, u32[]{:S(2)}) collective-permute-start(f32[3,2,2,128]{3,2,1,0:T(2,128)S(1)} %get-tuple-element.113), channel_id=1, source_target_pairs={{1,0},{2,1},{3,2},{4,3},{5,4},{6,5},{7,6},{9,8},{10,9},{11,10},{12... | collective-permute-start | bytes 18440 | tf_op jit(solution)/shard_map/ppermute | solution.py:23
  185.3 5.5 %collective-permute-start.9 = (f32[3,2,2,128]{3,2,1,0:T(2,128)S(1)}, f32[3,2,2,128]{3,2,1,0:T(2,128)S(1)}, u32[]{:S(2)}, u32[]{:S(2)}) collective-permute-start(f32[3,2,2,128]{3,2,1,0:T(2,128)S(1)} %get-tuple-element.112), channel_id=1, source_target_pairs={{0,1},{1,2},{2,3},{3,4},{4,5},{5,6},{6,7},{8,9},{9,10},{10,11},{11... | collective-permute-start | bytes 18440 | tf_op jit(solution)/shard_map/ppermute | solution.py:21
  196.5 23.4 %all-to-all-start.4 = ((f32[2,8,96]{2,0,1:T(2,128)}), f32[2,8,96]{2,0,1:T(2,128)S(1)}, u32[]{:S(2)}, u32[]{:S(2)}) async-start(f32[2,8,96]{2,0,1:T(2,128)} %pad_maximum_fusion.13), calls=%async_computation.4 | async-start | bytes 16384 | tf_op jit(solution)/shard_map/all_to_all | solution.py:129
  228.1 0.6 copy-start.14
  242.4 0.7 copy-start.15
